TPU v7x, 32 devices: a whole 2x2x4 slice. The times are simulated.
32 devices in a mesh: row: 4 (over x, core), col: 8 (over z, y).
Axes of the slice: x: 2, y: 2, z: 4, core: 2. Of those that a mesh axis runs over, the one named last changes fastest.
Arguments:
- signatures: bfloat16 [2048, 49152], P('row', 'col'), as said below
- trailing: float32 [2048, 1024], P('row', 'col'), may hold values from -6 to 6
- ridge: float32 [1], replicated, may hold values from 0.5 to 2
- panel_index: int32 [1], replicated, may hold values from 1 to 3
Outputs:
- factor: float32 [2048, 256], P(('row', 'col'))
- updated: float32 [2048, 1024], P('row', 'col')
Inputs may be any that keep to these rules, and one draw needn't show every extreme that they name: `signatures`: every diagonal block of the Gram matrix plus the ridge is positive definite.
All inputs are finite; a program needn't handle non-finite values.
Results may differ from a plain program's by a relative error of at most 0.0003.
Values may be sent and summed in bfloat16 or wider, within the bound.
A program may use at most 64 MiB of HBM per device.

v0:
```python
import jax
import jax.numpy as jnp
from jax import lax
from jax.sharding import PartitionSpec as P

PANEL = 256


def spread(block, axis, owner):
    block = jnp.where(lax.axis_index(axis) == owner, block, jnp.zeros_like(block))
    return lax.psum(block, axis)


def add_ridge(block, first_row, panel_start, ridge):
    row_ids = first_row + lax.broadcasted_iota(jnp.int32, block.shape, 0)
    col_ids = panel_start + lax.broadcasted_iota(jnp.int32, block.shape, 1)
    return block + jnp.where(row_ids == col_ids, ridge[0], jnp.zeros((), block.dtype))


def mask_above(block, first_row, panel_start):
    row_ids = first_row + lax.broadcasted_iota(jnp.int32, block.shape, 0)
    return jnp.where(row_ids >= panel_start, block, jnp.zeros((), block.dtype))


def solve_rows(lower, panel_rows):
    return jax.scipy.linalg.solve_triangular(lower, panel_rows.T, lower=True).T


def local(signatures, trailing, ridge, panel_index):
    rows_dev = signatures.shape[0]
    tile_cols = trailing.shape[1]
    col_count = lax.axis_size("col")
    row_share = rows_dev // col_count
    row_pos = lax.axis_index("row")
    col_pos = lax.axis_index("col")
    panel_start = panel_index[0] * PANEL
    row_owner = panel_start // rows_dev
    local_offset = panel_start % rows_dev
    own_paths = lax.dynamic_slice_in_dim(signatures, local_offset, PANEL, 0)
    panel_paths = spread(own_paths, "row", row_owner)
    mine_rows = lax.psum_scatter(
        lax.dot_general(
            signatures, panel_paths, (((1,), (1,)), ((), ())), preferred_element_type=jnp.float32
        ),
        "col",
        scatter_dimension=0,
        tiled=True,
    )
    mine_rows = add_ridge(mine_rows, row_pos * rows_dev + col_pos * row_share, panel_start, ridge)
    own_block = lax.dot_general(
        panel_paths, panel_paths, (((1,), (1,)), ((), ())), preferred_element_type=jnp.float32
    )
    diagonal = lax.psum(own_block, "col")
    diagonal = add_ridge(diagonal, panel_start, panel_start, ridge)
    lower = jnp.linalg.cholesky(diagonal)
    factor_mine = solve_rows(lower, mine_rows)
    factor_mine = mask_above(factor_mine, row_pos * rows_dev + col_pos * row_share, panel_start)
    factor_block = lax.all_gather(factor_mine, "col", axis=0, tiled=True)
    window_start = panel_start + PANEL + col_pos * tile_cols
    window_owner = window_start // rows_dev
    window_cut = lax.dynamic_slice_in_dim(factor_block, window_start % rows_dev, tile_cols, 0)
    window_rows = spread(window_cut, "row", window_owner)
    updated = trailing - lax.dot_general(
        factor_block,
        window_rows,
        (((1,), (1,)), ((), ())),
        precision=lax.Precision.HIGHEST,
        preferred_element_type=jnp.float32,
    )
    return (factor_mine, updated)


def solution(mesh):
    placed = (P("row", "col"), P("row", "col"), P(), P())
    return jax.shard_map(
        local,
        mesh=mesh,
        in_specs=placed,
        out_specs=(P(("row", "col"), None), P("row", "col")),
        check_vma=False,
    )
```

profile of v0, /device:TPU:9, one launch (start us, length us, event | category | flops | bytes accessed | tf_op | source)
XLA Modules:
  0.0 296.9 jit_solution(7277814875881397498)
XLA Ops:
  7.2 0.0 all-reduce.5.cloned.1.call-start
  7.9 4.5 %dynamic-slice_select_fusion = bf16[256,6144]{1,0:T(8,128)(2,1)} fusion(bf16[512,6144]{1,0:T(8,128)(2,1)} %param.4, s32[]{:T(128)S(6)} %select_n.62, pred[]{:T(512)S(6)} %eq.15), kind=kLoop, calls=%fused_computation.2 | loop fusion | flops 1572864 | bytes 6291461 | tf_op jit(solution)/shard_map/jit(_where)/select_n | solution.py:10
  12.4 0.0 all-reduce.5.cloned.1.call-update
  12.5 0.0 all-reduce.7.cloned.1.call-start
  13.3 68.7 %all-reduce.5.cloned.1.call-done = bf16[256,6144]{1,0:T(8,128)(2,1)} async-done(((bf16[256,6144]{1,0:T(8,128)(2,1)}), bf16[256,6144]{1,0:T(8,128)(2,1)}) %all-reduce.5.cloned.1.call-update) | async-done | bytes 3145744 | tf_op jit(solution)/shard_map/psum | solution.py:11
  81.9 4.6 %fusion.10 = f32[256,256]{0,1:T(8,128)} fusion(bf16[256,6144]{1,0:T(8,128)(2,1)} %all-reduce.5.cloned.1.call-done), kind=kOutput, calls=%fused_computation.39 | convolution fusion | flops 805306368 | bytes 3407872 | tf_op jit(solution)/shard_map/dot_general | solution.py:50
  86.5 0.0 all-reduce.7.cloned.1.call-update
  86.5 0.0 reduce-scatter.4.cloned.1.call-start
  86.6 5.6 %convolution_bitcast_fusion = f32[512,256]{0,1:T(8,128)S(1)} fusion(bf16[256,6144]{1,0:T(8,128)(2,1)} %all-reduce.5.cloned.1.call-done, bf16[512,6144]{1,0:T(8,128)(2,1)} %param.4), kind=kOutput, calls=%fused_computation.3 | convolution fusion | flops 1610612736 | bytes 9961472 | tf_op jit(solution)/shard_map/dot_general | solution.py:42
  92.1 1.0 copy.19
  93.1 0.0 reduce-scatter.4.cloned.1.call-update
  93.2 0.2 all-reduce.9.cloned.1.call-start
  93.4 62.0 %all-reduce.7.cloned.1.call-done = f32[256,256]{0,1:T(8,128)} async-done(((f32[256,256]{0,1:T(8,128)}), f32[256,256]{0,1:T(8,128)}) %all-reduce.7.cloned.1.call-update) | async-done | bytes 262160 | tf_op jit(solution)/shard_map/psum | solution.py:53
  155.4 1.0 select_add_fusion
  156.4 0.1 copy.13
  156.6 1.1 fusion
  157.7 11.7 %cholesky.49 = f32[128,128]{1,0:T(8,128)S(1)} custom-call(f32[128,128]{1,0:T(8,128)S(1)} %cholesky.115), custom_call_target="Cholesky" | custom-call | tf_op jit(solution)/shard_map/jit(cholesky)/cholesky | solution.py:55
  169.4 9.8 %custom-call.15 = f32[1,128,128]{1,2,0:T(8,128)S(1)} custom-call(f32[1,128,128]{2,1,0:T(8,128)S(1)} %get-tuple-element.29), custom_call_target="InvertDiagBlocksLowerTriangular" | custom-call | tf_op jit(solution)/shard_map/jit(cholesky)/cholesky | solution.py:55
  179.2 0.0 copy-start.1
  179.2 0.2 fusion.5
  179.5 0.3 convolution_subtract_fusion.2
  179.7 11.7 %cholesky.103 = f32[128,128]{1,0:T(8,128)S(1)} custom-call(f32[128,128]{1,0:T(8,128)S(1)} %convolution_subtract_fusion.2), custom_call_target="Cholesky" | custom-call | tf_op jit(solution)/shard_map/jit(cholesky)/cholesky | solution.py:55
  191.5 0.1 copy.16
  191.6 0.1 copy.15
  191.7 0.1 copy.14
  191.8 0.6 compare_reduce_fusion
  193.8 0.1 triangular_solve.60
  193.9 4.4 %while.1 = (s32[]{:T(128)}, f32[256,256]{0,1:T(8,128)S(1)}, s32[2,2]{1,0:T(2,128)S(1)}, f32[2,128,128]{2,1,0:T(8,128)S(1)}, s32[]{:T(128)}) while((s32[]{:T(128)}, f32[256,256]{0,1:T(8,128)S(1)}, s32[2,2]{1,0:T(2,128)S(1)}, f32[2,128,128]{2,1,0:T(8,128)S(1)}, s32[]{:T(128)}) %tuple.27), condition=%wide.while_cond, body=%wide.while_body.sunk | while | flops 2 | bytes 393321 | solution.py:26
  194.1 0.6 fusion.22
  194.7 1.4 dynamic-slice.7
  196.1 0.1 copy.23
  196.2 0.6 fusion.22
  196.8 1.4 dynamic-slice.7
  198.2 0.1 copy.23
  198.3 19.7 %custom-call.16 = f32[2,128,128]{1,2,0:T(8,128)S(1)} custom-call(f32[2,128,128]{2,1,0:T(8,128)S(1)} %get-tuple-element.9), custom_call_target="InvertDiagBlocksLowerTriangular" | custom-call | tf_op jit(solution)/shard_map/jit(_solve_triangular)/triangular_solve | solution.py:26
  218.0 4.0 %reduce-scatter.4.cloned.1.call-done = f32[64,256]{1,0:T(8,128)} async-done(((f32[512,256]{1,0:T(8,128)}), f32[64,256]{1,0:T(8,128)}) %reduce-scatter.4.cloned.1.call-update) | async-done | bytes 65552
  222.0 0.9 copy.20
  223.0 0.1 add_bitcast_fusion
  223.1 0.3 fusion.3
  223.3 0.3 convolution_subtract_fusion.1
  223.6 0.3 fusion.2
  223.9 0.1 fusion.7
  224.0 0.0 copy-start
  224.0 23.2 %all_gather.3 = f32[512,256]{1,0:T(8,128)S(1)} all-gather(f32[64,256]{1,0:T(8,128)S(1)} %fusion.7), channel_id=1, replica_groups=mesh['row'=4,'col'=8] {'col'}, dimensions={0}, use_global_device_ids=true | all-gather | bytes 589824 | tf_op jit(solution)/shard_map/all_gather | solution.py:58
  247.2 0.7 dynamic-slice_select_fusion.1
  247.9 0.0 all-reduce.9.cloned.1.call-update
  247.9 40.3 %all-reduce.9.cloned.1.call-done = f32[128,256]{1,0:T(8,128)} async-done(((f32[128,256]{1,0:T(8,128)}), f32[128,256]{1,0:T(8,128)}) %all-reduce.9.cloned.1.call-update) | async-done | bytes 131088 | tf_op jit(solution)/shard_map/psum | solution.py:11
  288.2 0.0 copy-done.1
  288.2 2.2 convolution_subtract_fusion
  290.4 0.0 copy-done
  (16 shorter events, 0.2 us)
Async XLA Ops:
  7.2 74.8 %all-reduce.5.cloned.1.call-start = ((), (), s32[]{:S(2)}) async-start(), calls=%async_computation.1 | async-start | bytes 6291456 | tf_op jit(solution)/shard_map/psum | solution.py:11
  12.5 142.9 %all-reduce.7.cloned.1.call-start = ((), (), s32[]{:S(2)}) async-start(), calls=%async_computation.2 | async-start | bytes 524288 | tf_op jit(solution)/shard_map/psum | solution.py:53
  86.5 135.5 %reduce-scatter.4.cloned.1.call-start = ((), (), s32[]{:S(2)}) async-start(), calls=%async_computation.4 | async-start | bytes 589824
  93.2 195.1 %all-reduce.9.cloned.1.call-start = ((), (), s32[]{:S(2)}) async-start(), calls=%async_computation.3 | async-start | bytes 262144 | tf_op jit(solution)/shard_map/psum | solution.py:11
  179.2 109.0 %copy-start.1 = (f32[512,128]{1,0:T(8,128)S(1)}, f32[512,128]{1,0:T(8,128)}, u32[]{:S(2)}) copy-start(f32[512,128]{1,0:T(8,128)} %param.5) | copy-start | bytes 786436
  224.0 66.4 %copy-start = (f32[64,256]{1,0:T(8,128)}, f32[64,256]{1,0:T(8,128)S(1)}, u32[]{:S(2)}) copy-start(f32[64,256]{1,0:T(8,128)S(1)} %fusion.7) | copy-start | bytes 196612
Sparse Core Ops, SparseCore 0:
  12.6 69.2 all-reduce.4
  86.6 68.7 all-reduce.6
  158.7 63.2 reduce-scatter.3
  248.1 40.0 all-reduce.8
where the time goes:
time: 300 us; the launch traced here: 297 us
  waiting for transfers between devices  175 us (58%)
  other arithmetic  61.2 us (20%)
  blocking collectives  23.2 us (8%)
  between operations  16.7 us (6%)
  matrix products  13.6 us (5%)
  local copies, waits for them, and re-layouts  6.6 us (2%)
    psum x2, waiting for transfers between devices, spread(): return lax.psum(block, axis)  109 us
    psum x1, waiting for transfers between devices, local(): diagonal = lax.psum(own_block, 'col')  62 us
    another operation x6, other arithmetic, local(): lower = jnp.linalg.cholesky(diagonal)  34 us
    all_gather x1, blocking collectives, local(): factor_block = lax.all_gather(factor_mine, 'col', axis=0, tiled=True)  23.2 us
    another operation x3, other arithmetic, solve_rows(): return jax.scipy.linalg.solve_triangular(lower, panel_rows.T, lower=True).T  19.7 us
  transfers between devices with their start and end apart: 4, of which 4 were waited for; matrix products, arithmetic and copies ran while one was open for 23% of the time, Pallas kernels for 0%

commit v1 on v0

v1 whole, which is shorter than its diff:
```python
import functools

import jax
import jax.numpy as jnp
from jax import lax
from jax.experimental import pallas as pl
from jax.experimental.pallas import tpu as pltpu
from jax.sharding import PartitionSpec as P

PANEL = 256
CORES = 2
MESH = pl.DeviceIdType.MESH
NT = (((1,), (1,)), ((), ()))
NN = (((1,), (0,)), ((), ()))


def remote(src, dst, send, recv, axis, where):
    return pltpu.make_async_remote_copy(
        src_ref=src, dst_ref=dst, send_sem=send, recv_sem=recv, device_id={axis: where}, device_id_type=MESH
    )


def gram_kernel(
    index, rows_count, col_count, steps, tile,
    sig_ref, gram_ref, window_ref, diagonal_ref,
    sig, panel, part, shares, block, win, diag,
    local_sem, p_send, p_recv, f_send, f_recv, rs_send, rs_recv, ag_send, ag_recv, w_send, w_recv, d_send, d_recv,
):
    rows, features = sig.shape
    half = PANEL // 2
    chunk = features // steps
    piece = chunk // CORES
    share = rows // col_count
    start = index * PANEL
    owner, offset = start // rows, start % rows
    owner_chip, owner_core = owner // CORES, owner % CORES
    row_pos, col_pos = lax.axis_index("row"), lax.axis_index("col")
    chip, core = row_pos // CORES, row_pos % CORES
    partner = chip * CORES + 1 - core
    is_owner = row_pos == owner
    is_mate = row_pos == owner_chip * CORES + 1 - owner_core
    is_far = chip != owner_chip

    load = pltpu.make_async_copy(sig_ref, sig, local_sem.at[0])
    load.start()
    barrier = pltpu.get_barrier_semaphore()
    for step in range(1, rows_count):
        pl.semaphore_signal(barrier, inc=1, device_id={"row": (row_pos + step) % rows_count}, device_id_type=MESH)
    for step in range(1, col_count):
        pl.semaphore_signal(barrier, inc=1, device_id={"col": (col_pos + step) % col_count}, device_id_type=MESH)
    pl.semaphore_wait(barrier, rows_count + col_count - 2)

    def panel_copy(h, k, slot, target, first, width):
        lanes = pl.ds(first, width)
        return remote(
            sig_ref.at[pl.ds(offset + h * half, half), lanes],
            panel.at[pl.ds(h * half, half), lanes],
            p_send.at[h, k, slot], p_recv.at[h, k], "row", target,
        )

    def owner_copies(h, k):
        copies = []
        for other in range(rows_count):
            if other // CORES != owner_chip:
                copies.append(panel_copy(h, k, other, other, k * chunk + other % CORES * piece, piece))
        copies.append(panel_copy(h, k, owner, owner_chip * CORES + 1 - owner_core, k * chunk, chunk))
        return copies

    def forward(h, k, which):
        first = pl.multiple_of(k * chunk + which * piece, 128)
        view = panel.at[pl.ds(h * half, half), pl.ds(first, piece)]
        return remote(view, view, f_send.at[h, k], f_recv.at[h, k], "row", partner)

    def half_load(h):
        return pltpu.make_async_copy(
            sig_ref.at[pl.ds(offset + h * half, half), :], panel.at[pl.ds(h * half, half), :], local_sem.at[1 + h]
        )

    @pl.when(is_owner)
    def _():
        for h in range(2):
            for k in range(steps):
                for copy in owner_copies(h, k):
                    copy.start()
        for h in range(2):
            half_load(h).start()

    def multiply(h):
        for k in range(steps):
            if k == 0:
                @pl.when(is_owner)
                def _():
                    half_load(h).wait()

            @pl.when(is_mate)
            def _():
                panel_copy(h, k, 0, 0, k * chunk, chunk).wait_recv()

            @pl.when(is_far)
            def _():
                panel_copy(h, k, 0, 0, pl.multiple_of(k * chunk + core * piece, 128), piece).wait_recv()
                forward(h, k, core).start()
                forward(h, k, 1 - core).wait_recv()

            lanes = pl.ds(k * chunk, chunk)
            product = lax.dot_general(
                sig[:, lanes], panel[pl.ds(h * half, half), lanes], NT, preferred_element_type=jnp.float32
            )
            if k == 0:
                part[h] = product
            else:
                part[h] += product
            if h == 1 and k == steps // 2 - 1:
                gather_start(0)

    def scatter(h, step):
        peer = (col_pos + step) % col_count
        return remote(
            part.at[h, pl.ds(pl.multiple_of(peer * share, share), share)], shares.at[h, step],
            rs_send.at[h, step], rs_recv.at[h, step], "col", peer,
        )

    def gather(h, step, shift):
        mine = pl.ds(pl.multiple_of((col_pos + shift) % col_count * share, share), share)
        return remote(
            block.at[h, mine], block.at[h, mine],
            ag_send.at[h, step], ag_recv.at[h, step], "col", (col_pos + step) % col_count,
        )

    def scatter_start(h):
        for step in range(1, col_count):
            scatter(h, step).start()

    def gather_start(h):
        mine = pl.ds(pl.multiple_of(col_pos * share, share), share)
        total = part[h, mine]
        for step in range(1, col_count):
            scatter(h, step).wait_recv()
            total += shares[h, step]
        block[h, mine] = total
        for step in range(1, col_count):
            gather(h, step, 0).start()

    window_first = start + PANEL + col_pos * tile
    window_owner = window_first // rows
    window_cut = pl.ds(pl.multiple_of(window_first % rows, tile), tile)
    diagonal_cut = pl.ds(offset, PANEL)

    def window_copy(h, step):
        return remote(
            block.at[h, window_cut], win.at[h], w_send.at[h, step], w_recv.at[h],
            "row", (row_pos + step) % rows_count,
        )

    def diagonal_copy(h, step):
        return remote(
            block.at[h, diagonal_cut], diag.at[h], d_send.at[h, step], d_recv.at[h],
            "row", (row_pos + step) % rows_count,
        )

    def spread(h):
        for step in range(1, col_count):
            gather(h, step, col_count - step).wait_recv()

        @pl.when(row_pos == window_owner)
        def _():
            for step in range(1, rows_count):
                window_copy(h, step).start()

        @pl.when(is_owner)
        def _():
            for step in range(1, rows_count):
                diagonal_copy(h, step).start()

        gram_ref[:, pl.ds(h * half, half)] = block[h]

    load.wait()
    multiply(0)
    scatter_start(0)
    multiply(1)
    scatter_start(1)
    spread(0)
    gather_start(1)
    spread(1)

    for h in range(2):
        lanes = pl.ds(h * half, half)

        @pl.when(row_pos == window_owner)
        def _():
            window_ref[:, lanes] = block[h, window_cut]

        @pl.when(row_pos != window_owner)
        def _():
            window_copy(h, 1).wait_recv()
            window_ref[:, lanes] = win[h]

        @pl.when(is_owner)
        def _():
            diagonal_ref[:, lanes] = block[h, diagonal_cut]

        @pl.when(row_pos != owner)
        def _():
            diagonal_copy(h, 1).wait_recv()
            diagonal_ref[:, lanes] = diag[h]

    for h in range(2):
        for step in range(1, col_count):
            scatter(h, step).wait_send()
            gather(h, step, 0).wait_send()

        @pl.when(is_owner)
        def _():
            for k in range(steps):
                for copy in owner_copies(h, k):
                    copy.wait_send()
            for step in range(1, rows_count):
                diagonal_copy(h, step).wait_send()

        @pl.when(is_far)
        def _():
            for k in range(steps):
                forward(h, k, core).wait_send()

        @pl.when(row_pos == window_owner)
        def _():
            for step in range(1, rows_count):
                window_copy(h, step).wait_send()


def gram_columns(index, rows_count, col_count, tile, signatures):
    rows, features = signatures.shape
    steps = max(n for n in range(1, 5) if features % (n * 128 * CORES) == 0)
    half = PANEL // 2
    dma = pltpu.SemaphoreType.DMA
    vmem = pl.BlockSpec(memory_space=pltpu.VMEM)
    return pl.pallas_call(
        functools.partial(gram_kernel, index, rows_count, col_count, steps, tile),
        name=f"gram_{index}",
        out_shape=[jax.ShapeDtypeStruct((n, PANEL), jnp.float32) for n in (rows, tile, PANEL)],
        in_specs=[pl.BlockSpec(memory_space=pl.ANY)],
        out_specs=[vmem] * 3,
        scratch_shapes=[
            pltpu.VMEM((rows, features), jnp.bfloat16),
            pltpu.VMEM((PANEL, features), jnp.bfloat16),
            pltpu.VMEM((2, rows, half), jnp.float32),
            pltpu.VMEM((2, col_count, rows // col_count, half), jnp.float32),
            pltpu.VMEM((2, rows, half), jnp.float32),
            pltpu.VMEM((2, tile, half), jnp.float32),
            pltpu.VMEM((2, PANEL, half), jnp.float32),
            dma((3,)),
            dma((2, steps, rows_count)), dma((2, steps)),
            dma((2, steps)), dma((2, steps)),
            dma((2, col_count)), dma((2, col_count)),
            dma((2, col_count)), dma((2, col_count)),
            dma((2, rows_count)), dma((2,)),
            dma((2, rows_count)), dma((2,)),
        ],
        compiler_params=pltpu.CompilerParams(
            collective_id=index, has_side_effects=True, vmem_limit_bytes=40 * 1024 * 1024
        ),
    )(signatures)


def dot(a, b, dims):
    return lax.dot_general(a, b, dims, precision=lax.Precision.HIGHEST, preferred_element_type=jnp.float32)


def invert_factor(work):
    size = work.shape[0]
    row_ids = lax.broadcasted_iota(jnp.int32, (size, size), 0)
    col_ids = lax.broadcasted_iota(jnp.int32, (size, size), 1)

    def step(k, _):
        value = work[...]
        pivot_row = work[pl.ds(k, 1), :]
        at_k = col_ids == k
        column = jnp.sum(jnp.where(at_k, value, 0.0), axis=1, keepdims=True)
        pivot = jnp.sum(jnp.where(at_k[:1], pivot_row, 0.0), axis=1, keepdims=True)
        scale = jnp.where(row_ids[:, :1] > k, column / pivot, 0.0)
        base = jnp.where(at_k & (row_ids > k), 0.0, value)
        work[...] = base - scale * jnp.where(at_k[:1], 1.0, pivot_row)
        return 0

    lax.fori_loop(0, size, step, 0)
    value = work[...]
    same = row_ids == col_ids
    pivots = jnp.sum(jnp.where(same, value, 0.0), axis=1, keepdims=True)
    unit = jnp.where(row_ids > col_ids, value, jnp.where(same, 1.0, 0.0))
    return unit / jnp.sqrt(pivots)


def update_kernel(
    index_ref, ridge_ref, gram_ref, window_ref, diagonal_ref, trailing_ref, factor_ref, updated_ref, work, inverse, full
):
    rows = gram_ref.shape[0]
    share = factor_ref.shape[0]
    half = PANEL // 2
    start = index_ref[0] * PANEL
    ridge = ridge_ref[0]
    first_row = index_ref[1] * rows
    row_ids = lax.broadcasted_iota(jnp.int32, (half, half), 0)
    col_ids = lax.broadcasted_iota(jnp.int32, (half, half), 1)
    ridge_block = jnp.where(row_ids == col_ids, ridge, 0.0)
    work[...] = diagonal_ref[:half, :half] + ridge_block
    first = invert_factor(work)
    below = dot(diagonal_ref[half:, :half], first, NT)
    work[...] = diagonal_ref[half:, half:] + ridge_block - dot(below, below, NT)
    second = invert_factor(work)
    inverse[:half, :half] = first
    inverse[:half, half:] = jnp.zeros((half, half), jnp.float32)
    inverse[half:, half:] = second
    inverse[half:, :half] = -dot(second, dot(below, first, NN), NN)
    ids = first_row + lax.broadcasted_iota(jnp.int32, (rows, PANEL), 0)
    panel_ids = start + lax.broadcasted_iota(jnp.int32, (rows, PANEL), 1)
    gram = gram_ref[...] + jnp.where(ids == panel_ids, ridge, 0.0)
    full[...] = jnp.where(ids >= start, dot(gram, inverse[...], NT), 0.0)
    window = dot(window_ref[...], inverse[...], NT)
    updated_ref[...] = trailing_ref[...] - dot(full[...], window, NT)
    factor_ref[...] = full[pl.ds(pl.multiple_of(index_ref[2] * share, share), share), :]


def update(places, ridge, gram, window, diagonal, trailing, share):
    vmem = pl.BlockSpec(memory_space=pltpu.VMEM)
    smem = pl.BlockSpec(memory_space=pltpu.SMEM)
    half = PANEL // 2
    return pl.pallas_call(
        update_kernel,
        name="update",
        out_shape=[
            jax.ShapeDtypeStruct((share, PANEL), jnp.float32),
            jax.ShapeDtypeStruct(trailing.shape, jnp.float32),
        ],
        in_specs=[smem, smem] + [vmem] * 4,
        out_specs=[vmem] * 2,
        scratch_shapes=[
            pltpu.VMEM((half, half), jnp.float32),
            pltpu.VMEM((PANEL, PANEL), jnp.float32),
            pltpu.VMEM(gram.shape, jnp.float32),
        ],
        compiler_params=pltpu.CompilerParams(vmem_limit_bytes=40 * 1024 * 1024),
    )(places, ridge, gram, window, diagonal, trailing)


def solution(mesh):
    rows_count, col_count = mesh.shape["row"], mesh.shape["col"]

    def local(signatures, trailing, ridge, panel_index):
        rows, tile = signatures.shape[0], trailing.shape[1]
        panels = (rows * rows_count - tile * col_count) // PANEL
        branches = [
            functools.partial(gram_columns, index, rows_count, col_count, tile) for index in range(1, panels)
        ]
        gram, window, diagonal = lax.switch(panel_index[0] - 1, branches, signatures)
        places = jnp.stack([panel_index[0], lax.axis_index("row"), lax.axis_index("col")]).astype(jnp.int32)
        return tuple(update(places, ridge, gram, window, diagonal, trailing, rows // col_count))

    return jax.shard_map(
        local,
        mesh=mesh,
        in_specs=(P("row", "col"), P("row", "col"), P(), P()),
        out_specs=(P(("row", "col"), None), P("row", "col")),
        check_vma=False,
    )
```

time: 300 us -> 93 us (0.31)
  waiting for transfers between devices: 175 us -> 0 us
  Pallas kernels: 0 us -> 90.2 us
  other arithmetic: 61.2 us -> 0.08 us
  blocking collectives: 23.2 us -> 0 us
  between operations: 16.7 us -> 1.96 us
  matrix products: 13.6 us -> 0 us
  local copies, waits for them, and re-layouts: 6.6 us -> 0.01 us
    psum x3 -> x0, waiting for transfers between devices: 171 us -> none  [the longest x2 109 us: spread(): return lax.psum(block, axis)]
    pallas_call x0 -> x2, Pallas kernels: none -> 90.2 us  [the longest x1 60.2 us: gram_columns(): pl.pallas_call(functools.partial(gram_kernel, index, rows_count, col_coun...]
    another operation x9 -> x1, other arithmetic: 53.7 us -> 0.08 us  [local(): jnp.stack([panel_index[0], lax.axis_index('row'), lax.axis_index('col')])]
    all_gather x1 -> x0, blocking collectives: 23.2 us -> none  [local(): factor_block = lax.all_gather(factor_mine, 'col', axis=0, tiled=True)]
    dot_general x3 -> x0, matrix products: 12.3 us -> none  [the longest x1 5.57 us: local(): lax.dot_general(signatures, panel_paths, (((1,), (1,)), ((), ())), prefer...]
    select_n x3 -> x0, other arithmetic: 5.29 us -> none  [the longest x2 5.21 us: spread(): jnp.where(lax.axis_index(axis) == owner, block, jnp.zeros_like(block))]
    another operation x18 -> x0, local copies, waits for them, and re-layouts: 4.54 us -> none
    unnamed x5 -> x0, waiting for transfers between devices: 4.1 us -> none
  transfers between devices with their start and end apart: 4 -> 0, of which waited for: 4 -> 0; matrix products, arithmetic and copies ran while one was open for 23% -> 0% of each run, Pallas kernels for 0% -> 0%
where the time goes in v1:
time: 93 us; the launch traced here: 92.2 us
  Pallas kernels  90.2 us (97%)
  between operations  1.96 us (2%)
    pallas_call x1, Pallas kernels, gram_columns(): pl.pallas_call(functools.partial(gram_kernel, index, rows_count, col_coun...  60.2 us
    pallas_call x1, Pallas kernels, update(): pl.pallas_call(update_kernel, name='update', out_shape=[jax.ShapeDtypeStr...  30 us

profile of v1, /device:TPU:9, one launch (start us, length us, event | category | flops | bytes accessed | tf_op | source)
XLA Modules:
  0.0 92.2 jit_solution(4699526350968436775)
XLA Ops:
  1.3 0.0 copy-start
  1.3 60.2 %conditional.1 = ((f32[512,256]{1,0:T(8,128)S(1)}, f32[128,256]{1,0:T(8,128)S(1)}, f32[256,256]{1,0:T(8,128)S(1)})) conditional(s32[]{:T(128)} %bitcast.2, bf16[512,6144]{1,0:T(8,128)(2,1)} %param.7, bf16[512,6144]{1,0:T(8,128)(2,1)} %param.7, bf16[512,6144]{1,0:T(8,128)(2,1)} %param.7), branch_computations={%region_0.0_spmd, %region_1.0_spmd, %region_2.0_spmd} | conditional | bytes 8 | solution.py:354
  1.3 60.2 %gram_2.1 = (f32[512,256]{1,0:T(8,128)S(1)}, f32[128,256]{1,0:T(8,128)S(1)}, f32[256,256]{1,0:T(8,128)S(1)}) custom-call(bf16[512,6144]{1,0:T(8,128)(2,1)} %sig_ref.1), custom_call_target="tpu_custom_call" | custom-call | tf_op jit(solution)/shard_map/cond/branch_1_fun/gram_2/pallas_call | solution.py:237
  61.5 0.1 pad_add_fusion.index_ref
  62.3 0.0 copy-done
  62.3 30.0 %update.1 = (f32[64,256]{1,0:T(8,128)}, f32[512,128]{1,0:T(8,128)}) custom-call(s32[3]{0:T(128)S(1)} %pad_add_fusion.index_ref, f32[1]{0:T(128)S(6)} %copy.15.ridge_ref, f32[512,256]{1,0:T(8,128)S(1)} %get-tuple-element.8.gram_ref, f32[128,256]{1,0:T(8,128)S(1)} %get-tuple-element.9.window_ref, f32[256,256]{1,0:T(8,128)S(1)} %get-tuple-element.10.diagonal_ref, ...), custom_call_target="tpu_custom_call" | custom-call | tf_op jit(solution)/shard_map/update/pallas_call | solution.py:327
Async XLA Ops:
  1.3 61.0 %copy-start = (f32[512,128]{1,0:T(8,128)S(1)}, f32[512,128]{1,0:T(8,128)}, u32[]{:S(2)}) copy-start(f32[512,128]{1,0:T(8,128)} %trailing_ref.1) | copy-start | bytes 786436

commit v2 on v1

--- a/solution.py
+++ b/solution.py
@@ -22,8 +22,8 @@
 
 def gram_kernel(
     index, rows_count, col_count, steps, tile,
-    sig_ref, gram_ref, window_ref, diagonal_ref,
-    sig, panel, part, shares, block, win, diag,
+    ridge_ref, sig_ref, gram_ref, window_ref, inverse_ref,
+    sig, panel, part, shares, block, win, inverse, work, below,
     local_sem, p_send, p_recv, f_send, f_recv, rs_send, rs_recv, ag_send, ag_recv, w_send, w_recv, d_send, d_recv,
 ):
     rows, features = sig.shape
@@ -144,7 +144,6 @@
     window_first = start + PANEL + col_pos * tile
     window_owner = window_first // rows
     window_cut = pl.ds(pl.multiple_of(window_first % rows, tile), tile)
-    diagonal_cut = pl.ds(offset, PANEL)
 
     def window_copy(h, step):
         return remote(
@@ -152,11 +151,28 @@
             "row", (row_pos + step) % rows_count,
         )
 
-    def diagonal_copy(h, step):
-        return remote(
-            block.at[h, diagonal_cut], diag.at[h], d_send.at[h, step], d_recv.at[h],
-            "row", (row_pos + step) % rows_count,
-        )
+    def inverse_copy(h, step):
+        view = inverse.at[h, pl.ds(h * half, PANEL - h * half)]
+        return remote(
+            view, view, d_send.at[h, step], d_recv.at[h], "row", (row_pos + step) % rows_count,
+        )
+
+    row_ids = lax.broadcasted_iota(jnp.int32, (half, half), 0)
+    col_ids = lax.broadcasted_iota(jnp.int32, (half, half), 1)
+    upper, lower = pl.ds(offset, half), pl.ds(offset + half, half)
+
+    def invert_first():
+        work[...] = block[0, upper] + jnp.where(row_ids == col_ids, ridge_ref[0], 0.0)
+        first = invert_factor(work)
+        inverse[0, :half] = first
+        below[...] = dot(block[0, lower], first, NT)
+
+    def invert_second():
+        ridge_block = jnp.where(row_ids == col_ids, ridge_ref[0], 0.0)
+        work[...] = block[1, lower] + ridge_block - dot(below[...], below[...], NT)
+        second = invert_factor(work)
+        inverse[1, half:] = second
+        inverse[0, half:] = -dot(second, dot(below[...], inverse[0, :half], NN), NN)
 
     def spread(h):
         for step in range(1, col_count):
@@ -166,11 +182,6 @@
         def _():
             for step in range(1, rows_count):
                 window_copy(h, step).start()
-
-        @pl.when(is_owner)
-        def _():
-            for step in range(1, rows_count):
-                diagonal_copy(h, step).start()
 
         gram_ref[:, pl.ds(h * half, half)] = block[h]
 
@@ -181,7 +192,15 @@
     scatter_start(1)
     spread(0)
     gather_start(1)
+    pl.when(is_owner)(invert_first)
     spread(1)
+
+    @pl.when(is_owner)
+    def _():
+        invert_second()
+        for h in range(2):
+            for step in range(1, rows_count):
+                inverse_copy(h, step).start()
 
     for h in range(2):
         lanes = pl.ds(h * half, half)
@@ -195,14 +214,13 @@
             window_copy(h, 1).wait_recv()
             window_ref[:, lanes] = win[h]
 
-        @pl.when(is_owner)
-        def _():
-            diagonal_ref[:, lanes] = block[h, diagonal_cut]
-
         @pl.when(row_pos != owner)
         def _():
-            diagonal_copy(h, 1).wait_recv()
-            diagonal_ref[:, lanes] = diag[h]
+            inverse_copy(h, 1).wait_recv()
+
+    inverse_ref[:, :half] = inverse[0]
+    inverse_ref[half:, half:] = inverse[1, half:]
+    inverse_ref[:half, half:] = jnp.zeros((half, half), jnp.float32)
 
     for h in range(2):
         for step in range(1, col_count):
@@ -215,7 +233,7 @@
                 for copy in owner_copies(h, k):
                     copy.wait_send()
             for step in range(1, rows_count):
-                diagonal_copy(h, step).wait_send()
+                inverse_copy(h, step).wait_send()
 
         @pl.when(is_far)
         def _():
@@ -228,7 +246,7 @@
                 window_copy(h, step).wait_send()
 
 
-def gram_columns(index, rows_count, col_count, tile, signatures):
+def gram_columns(index, rows_count, col_count, tile, ridge, signatures):
     rows, features = signatures.shape
     steps = max(n for n in range(1, 5) if features % (n * 128 * CORES) == 0)
     half = PANEL // 2
@@ -238,7 +256,7 @@
         functools.partial(gram_kernel, index, rows_count, col_count, steps, tile),
         name=f"gram_{index}",
         out_shape=[jax.ShapeDtypeStruct((n, PANEL), jnp.float32) for n in (rows, tile, PANEL)],
-        in_specs=[pl.BlockSpec(memory_space=pl.ANY)],
+        in_specs=[pl.BlockSpec(memory_space=pltpu.SMEM), pl.BlockSpec(memory_space=pl.ANY)],
         out_specs=[vmem] * 3,
         scratch_shapes=[
             pltpu.VMEM((rows, features), jnp.bfloat16),
@@ -248,6 +266,8 @@
             pltpu.VMEM((2, rows, half), jnp.float32),
             pltpu.VMEM((2, tile, half), jnp.float32),
             pltpu.VMEM((2, PANEL, half), jnp.float32),
+            pltpu.VMEM((half, half), jnp.float32),
+            pltpu.VMEM((half, half), jnp.float32),
             dma((3,)),
             dma((2, steps, rows_count)), dma((2, steps)),
             dma((2, steps)), dma((2, steps)),
@@ -259,7 +279,7 @@
         compiler_params=pltpu.CompilerParams(
             collective_id=index, has_side_effects=True, vmem_limit_bytes=40 * 1024 * 1024
         ),
-    )(signatures)
+    )(ridge, signatures)
 
 
 def dot(a, b, dims):
@@ -268,62 +288,69 @@
 
 def invert_factor(work):
     size = work.shape[0]
+    segment = size // 4
+
+    def pick(mask, value):
+        return jnp.sum(jnp.where(mask, value, 0.0), axis=1, keepdims=True)
+
+    for top in range(0, size, segment):
+        active = size - top
+        rows = top + lax.broadcasted_iota(jnp.int32, (active, 1), 0)
+        lanes = lax.broadcasted_iota(jnp.int32, (active, size), 1)
+        lane = lax.broadcasted_iota(jnp.int32, (1, size), 1)
+
+        def pair(i, _):
+            k = top + 2 * i
+            value = work[top:, :]
+            row_0, row_1 = work[pl.ds(k, 1), :], work[pl.ds(k + 1, 1), :]
+            at_0, at_1 = lane == k, lane == k + 1
+            column_0 = pick(lanes == k, value)
+            column_1 = pick(lanes == k + 1, value)
+            cross = pick(at_1, row_0)
+            over_0 = 1.0 / pick(at_0, row_0)
+            ratio = pick(at_0, row_1) * over_0
+            over_1 = 1.0 / (pick(at_1, row_1) - ratio * cross)
+            unit_0 = jnp.where(at_0, 1.0, row_0)
+            next_1 = jnp.where(at_0, 0.0, row_1) - ratio * unit_0
+            later = rows > k + 1
+            scale_0 = jnp.where(later, column_0 * over_0, 0.0)
+            scale_1 = jnp.where(later, (column_1 - scale_0 * cross) * over_1, 0.0)
+            base = jnp.where(later & ((lanes == k) | (lanes == k + 1)), 0.0, value)
+            work[top:, :] = (
+                base - scale_0 * jnp.where(at_1, 0.0, unit_0) - scale_1 * jnp.where(at_1, 1.0, next_1)
+            )
+            work[pl.ds(k + 1, 1), :] = next_1
+            return 0
+
+        lax.fori_loop(0, segment // 2, pair, 0)
     row_ids = lax.broadcasted_iota(jnp.int32, (size, size), 0)
     col_ids = lax.broadcasted_iota(jnp.int32, (size, size), 1)
-
-    def step(k, _):
-        value = work[...]
-        pivot_row = work[pl.ds(k, 1), :]
-        at_k = col_ids == k
-        column = jnp.sum(jnp.where(at_k, value, 0.0), axis=1, keepdims=True)
-        pivot = jnp.sum(jnp.where(at_k[:1], pivot_row, 0.0), axis=1, keepdims=True)
-        scale = jnp.where(row_ids[:, :1] > k, column / pivot, 0.0)
-        base = jnp.where(at_k & (row_ids > k), 0.0, value)
-        work[...] = base - scale * jnp.where(at_k[:1], 1.0, pivot_row)
-        return 0
-
-    lax.fori_loop(0, size, step, 0)
     value = work[...]
     same = row_ids == col_ids
-    pivots = jnp.sum(jnp.where(same, value, 0.0), axis=1, keepdims=True)
     unit = jnp.where(row_ids > col_ids, value, jnp.where(same, 1.0, 0.0))
-    return unit / jnp.sqrt(pivots)
+    return unit / jnp.sqrt(pick(same, value))
 
 
 def update_kernel(
-    index_ref, ridge_ref, gram_ref, window_ref, diagonal_ref, trailing_ref, factor_ref, updated_ref, work, inverse, full
+    index_ref, ridge_ref, gram_ref, window_ref, inverse_ref, trailing_ref, factor_ref, updated_ref, full
 ):
     rows = gram_ref.shape[0]
     share = factor_ref.shape[0]
-    half = PANEL // 2
     start = index_ref[0] * PANEL
     ridge = ridge_ref[0]
     first_row = index_ref[1] * rows
-    row_ids = lax.broadcasted_iota(jnp.int32, (half, half), 0)
-    col_ids = lax.broadcasted_iota(jnp.int32, (half, half), 1)
-    ridge_block = jnp.where(row_ids == col_ids, ridge, 0.0)
-    work[...] = diagonal_ref[:half, :half] + ridge_block
-    first = invert_factor(work)
-    below = dot(diagonal_ref[half:, :half], first, NT)
-    work[...] = diagonal_ref[half:, half:] + ridge_block - dot(below, below, NT)
-    second = invert_factor(work)
-    inverse[:half, :half] = first
-    inverse[:half, half:] = jnp.zeros((half, half), jnp.float32)
-    inverse[half:, half:] = second
-    inverse[half:, :half] = -dot(second, dot(below, first, NN), NN)
     ids = first_row + lax.broadcasted_iota(jnp.int32, (rows, PANEL), 0)
     panel_ids = start + lax.broadcasted_iota(jnp.int32, (rows, PANEL), 1)
     gram = gram_ref[...] + jnp.where(ids == panel_ids, ridge, 0.0)
-    full[...] = jnp.where(ids >= start, dot(gram, inverse[...], NT), 0.0)
-    window = dot(window_ref[...], inverse[...], NT)
+    full[...] = jnp.where(ids >= start, dot(gram, inverse_ref[...], NT), 0.0)
+    window = dot(window_ref[...], inverse_ref[...], NT)
     updated_ref[...] = trailing_ref[...] - dot(full[...], window, NT)
     factor_ref[...] = full[pl.ds(pl.multiple_of(index_ref[2] * share, share), share), :]
 
 
-def update(places, ridge, gram, window, diagonal, trailing, share):
+def update(places, ridge, gram, window, inverse, trailing, share):
     vmem = pl.BlockSpec(memory_space=pltpu.VMEM)
     smem = pl.BlockSpec(memory_space=pltpu.SMEM)
-    half = PANEL // 2
     return pl.pallas_call(
         update_kernel,
         name="update",
@@ -333,13 +360,9 @@
         ],
         in_specs=[smem, smem] + [vmem] * 4,
         out_specs=[vmem] * 2,
-        scratch_shapes=[
-            pltpu.VMEM((half, half), jnp.float32),
-            pltpu.VMEM((PANEL, PANEL), jnp.float32),
-            pltpu.VMEM(gram.shape, jnp.float32),
-        ],
+        scratch_shapes=[pltpu.VMEM(gram.shape, jnp.float32)],
         compiler_params=pltpu.CompilerParams(vmem_limit_bytes=40 * 1024 * 1024),
-    )(places, ridge, gram, window, diagonal, trailing)
+    )(places, ridge, gram, window, inverse, trailing)
 
 
 def solution(mesh):
@@ -351,9 +374,9 @@
         branches = [
             functools.partial(gram_columns, index, rows_count, col_count, tile) for index in range(1, panels)
         ]
-        gram, window, diagonal = lax.switch(panel_index[0] - 1, branches, signatures)
+        gram, window, inverse = lax.switch(panel_index[0] - 1, branches, ridge, signatures)
         places = jnp.stack([panel_index[0], lax.axis_index("row"), lax.axis_index("col")]).astype(jnp.int32)
-        return tuple(update(places, ridge, gram, window, diagonal, trailing, rows // col_count))
+        return tuple(update(places, ridge, gram, window, inverse, trailing, rows // col_count))
 
     return jax.shard_map(
         local,

time: 93 us -> 67.6 us (0.73)
  Pallas kernels: 90.2 us -> 64 us
    pallas_call x1, Pallas kernels: 30 us -> 3.13 us  [update(): pl.pallas_call(update_kernel, name='update', out_shape=[jax.ShapeDtypeStr...]
where the time goes in v2:
time: 67.6 us; the launch traced here: 66.3 us
  Pallas kernels  64 us (95%)
  between operations  1.96 us (3%)
    pallas_call x1, Pallas kernels, gram_columns(): pl.pallas_call(functools.partial(gram_kernel, index, rows_count, col_coun...  60.9 us
    pallas_call x1, Pallas kernels, update(): pl.pallas_call(update_kernel, name='update', out_shape=[jax.ShapeDtypeStr...  3.13 us

profile of v2, /device:TPU:9, one launch (start us, length us, event | category | flops | bytes accessed | tf_op | source)
XLA Modules:
  0.0 66.3 jit_solution(11962265380649879268)
XLA Ops:
  1.3 0.0 copy-start
  1.3 61.1 %conditional.1 = ((f32[512,256]{1,0:T(8,128)S(1)}, f32[128,256]{1,0:T(8,128)S(1)}, f32[256,256]{1,0:T(8,128)S(1)})) conditional(s32[]{:T(128)} %bitcast.2, (f32[1]{0:T(128)}, bf16[512,6144]{1,0:T(8,128)(2,1)}) %tuple.16, (f32[1]{0:T(128)}, bf16[512,6144]{1,0:T(8,128)(2,1)}) %tuple.16, (f32[1]{0:T(128)}, ...), branch_computations={%region_0.0_spmd, %region_1.0_spmd, %region_2.0_spmd} | conditional | bytes 8 | solution.py:377
  1.3 60.9 %gram_3.1 = (f32[512,256]{1,0:T(8,128)S(1)}, f32[128,256]{1,0:T(8,128)S(1)}, f32[256,256]{1,0:T(8,128)S(1)}) custom-call(f32[1]{0:T(128)} %get-tuple-element.16.ridge_ref, bf16[512,6144]{1,0:T(8,128)(2,1)} %get-tuple-element.17.sig_ref), custom_call_target="tpu_custom_call" | custom-call | tf_op jit(solution)/shard_map/cond/branch_2_fun/gram_3/pallas_call | solution.py:255
  62.4 0.1 pad_add_fusion.index_ref
  63.2 0.0 copy-done
  63.2 3.1 %update.1 = (f32[64,256]{1,0:T(8,128)}, f32[512,128]{1,0:T(8,128)}) custom-call(s32[3]{0:T(128)S(1)} %pad_add_fusion.index_ref, f32[1]{0:T(128)S(6)} %copy.15.ridge_ref, f32[512,256]{1,0:T(8,128)S(1)} %get-tuple-element.23.gram_ref, f32[128,256]{1,0:T(8,128)S(1)} %get-tuple-element.24.window_ref, f32[256,256]{1,0:T(8,128)S(1)} %get-tuple-element.25.inverse_ref, ...), custom_call_target="tpu_custom_call" | custom-call | tf_op jit(solution)/shard_map/update/pallas_call | solution.py:354
Async XLA Ops:
  1.3 61.9 %copy-start = (f32[512,128]{1,0:T(8,128)S(1)}, f32[512,128]{1,0:T(8,128)}, u32[]{:S(2)}) copy-start(f32[512,128]{1,0:T(8,128)} %trailing_ref.1) | copy-start | bytes 786436
